TPU v7x, 32 devices: a whole 2x2x4 slice. The times are simulated.
32 devices in a mesh: space: 8 (over z, x), orb: 4 (over y, core).
Axes of the slice: x: 2, y: 2, z: 4, core: 2. Of those that a mesh axis runs over, the one named last changes fastest.
Arguments:
- psi: bfloat16 [16, 48, 48, 512], P('space', None, None, 'orb'), may hold values from -6 to 6
- potential: float32 [16, 48, 48], P('space'), may hold values from 0 to 2
- beta: bfloat16 [8, 16, 48, 48], P(None, 'space'), may hold values from -0.21875 to 0.21875
- strength: float32 [8], replicated, may hold values from 0.5 to 4
- atom_slab: int32 [8], replicated, may hold values from 0 to 7, each once
- pattern: int32 [12, 2], replicated, may hold values from 0 to 3, as said below
- q_tiles: bfloat16 [12, 128, 128], replicated, may hold values from -0.3125 to 0.3125
Outputs:
- rotated: bfloat16 [16, 48, 48, 512], P('space', None, None, 'orb')
Inputs may be any that keep to these rules, and one draw needn't show every extreme that they name: `pattern`: the 12 tile coordinates are distinct, each in 0 to 3, and every diagonal tile is among them.
All inputs are finite; a program needn't handle non-finite values.
Results may differ from a plain program's by a relative error of at most 0.0064.
Values may be sent and summed in bfloat16 or wider, within the bound.
No kernel may reach another device: no remote copies, remote signals or barrier semaphores. Data moves between devices by JAX's collectives and lax.ppermute only.
A program may use at most 64 MiB of HBM per device.

v0:
```python
import jax
import jax.numpy as jnp
from jax import lax
from jax.sharding import PartitionSpec as P


def passed_along(array, axis, by):
    length = lax.axis_size(axis)
    pairs = [(i, i + by) for i in range(length) if 0 <= i + by < length]
    return lax.ppermute(array, axis, pairs)


def with_halo(block, sides, width):
    for axis, dim in sides:
        count = lax.axis_size(axis)
        forward = [(i, i + 1) for i in range(count - 1)]
        backward = [(target, source) for source, target in forward]
        low = lax.ppermute(
            lax.slice_in_dim(block, block.shape[dim] - width, None, axis=dim), axis, forward
        )
        high = lax.ppermute(lax.slice_in_dim(block, 0, width, axis=dim), axis, backward)
        block = jnp.concatenate([low, block, high], axis=dim)
    return block


def gather_partials(partial_proj):
    proj = partial_proj
    proj = proj + passed_along(partial_proj, "space", 1)
    proj = proj + passed_along(partial_proj, "space", -1)
    proj = proj + passed_along(partial_proj, "space", 2)
    proj = proj + passed_along(partial_proj, "space", -2)
    return proj


def apply_filter(v2, planes, potential_flat, beta_m, strength):
    f = planes.astype(jnp.float32)
    padded = with_halo(planes, (("space", 0),), 1).astype(jnp.float32)
    pxy = jnp.pad(f, ((0, 0), (1, 1), (1, 1), (0, 0)))
    beside = padded[2:] + padded[:-2]
    beside = beside + pxy[:, 2:, 1:-1] + pxy[:, :-2, 1:-1] + pxy[:, 1:-1, 2:] + pxy[:, 1:-1, :-2]
    kinetic = -0.5 * (beside - 6.0 * f)
    partial_proj = jnp.dot(beta_m, v2, preferred_element_type=jnp.float32)
    proj = gather_partials(partial_proj)
    coef = (strength[:, None] * proj).astype(jnp.bfloat16)
    nonlocal_term = lax.dot_general(
        beta_m, coef, (((0,), (0,)), ((), ())), preferred_element_type=jnp.float32
    )
    total = (
        kinetic.reshape(v2.shape) + potential_flat[:, None] * f.reshape(v2.shape) + nonlocal_term
    )
    return ((total - 4.0 * f.reshape(v2.shape)) / 4.0).astype(jnp.bfloat16)


def shards(psi, potential, beta, strength, atom_slab, pattern, q_tiles):
    planes_z, width_x, width_y, orb_cols = psi.shape
    cells = planes_z * width_x * width_y
    my_slab = lax.axis_index("space")
    active = jnp.abs(my_slab - atom_slab) <= 1
    flat_beta = beta.reshape(beta.shape[0], cells)
    beta_m = jnp.where(active[:, None], flat_beta, jnp.zeros_like(flat_beta))
    potential_flat = potential.reshape(cells)
    first = apply_filter(psi.reshape(cells, orb_cols), psi, potential_flat, beta_m, strength)
    second = apply_filter(
        first, first.reshape(planes_z, width_x, width_y, orb_cols), potential_flat, beta_m, strength
    )
    tile = q_tiles.shape[1]
    blocks = orb_cols * lax.axis_size("orb") // tile
    my_col = lax.axis_index("orb")
    ids = jnp.arange(blocks, dtype=jnp.int32)
    rows_hot = (pattern[:, 0][:, None] == ids[None, :]).astype(jnp.float32)
    mine = (pattern[:, 1] == my_col).astype(jnp.float32)
    column_q = jnp.einsum("ki,k,kab->iab", rows_hot, mine, q_tiles.astype(jnp.float32))
    column_q = column_q.reshape(blocks * tile, tile).astype(jnp.bfloat16)
    result = jnp.dot(
        lax.all_gather(second, "orb", axis=1, tiled=True),
        column_q,
        preferred_element_type=jnp.float32,
    )
    return result.astype(jnp.bfloat16).reshape(planes_z, width_x, width_y, orb_cols)


def solution(mesh):
    placed = (
        P("space", None, None, "orb"),
        P("space", None, None),
        P(None, "space", None, None),
        P(),
        P(),
        P(),
        P(),
    )
    return jax.shard_map(
        shards, mesh=mesh, in_specs=placed, out_specs=P("space", None, None, "orb"), check_vma=False
    )
```

profile of v0, /device:TPU:0, one launch (start us, length us, event | category | flops | bytes accessed | tf_op | source)
XLA Modules:
  0.0 137.3 jit_solution(8860781879933464515)
XLA Ops:
  6.5 0.0 copy-start
  6.5 0.0 copy-start.7
  6.5 0.0 copy-start.2
  6.5 0.0 all-gather.2.cloned.1.call-start
  6.5 2.5 %fusion.30 = (bf16[1,48,48,128]{3,2,1,0:T(8,128)(2,1)}, bf16[1,48,48,128]{3,2,1,0:T(8,128)(2,1)}) fusion(bf16[2,48,48,128]{3,2,1,0:T(8,128)(2,1)} %param.7), kind=kLoop, calls=%fused_computation.59 | loop fusion | bytes 2359296 | tf_op jit(solution)/shard_map/slice | solution.py:19
  9.0 5.7 %collective-permute-start = (bf16[1,48,48,128]{3,2,1,0:T(8,128)(2,1)}, bf16[1,48,48,128]{3,2,1,0:T(8,128)(2,1)}, u32[]{:S(2)}, u32[]{:S(2)}) collective-permute-start(bf16[1,48,48,128]{3,2,1,0:T(8,128)(2,1)} %get-tuple-element.9), channel_id=1, source_target_pairs={{0,4},{4,8},{8,12},{12,16},{16,20},{20,24},{24,28},{1,5},{5,9},{9,... | collective-permute-start | bytes 1769480 | tf_op jit(solution)/shard_map/ppermute | solution.py:18
  14.7 1.3 collective-permute-start.1
  16.0 0.0 copy-done.7
  16.0 0.0 copy-done.2
  16.0 0.1 broadcast_select_fusion
  16.1 0.0 copy-done
  16.1 0.6 convolution_bitcast_fusion
  16.7 4.5 %collective-permute-start.2 = (f32[8,128]{1,0:T(8,128)S(1)}, f32[8,128]{1,0:T(8,128)S(1)}, u32[]{:S(2)}, u32[]{:S(2)}) collective-permute-start(f32[8,128]{1,0:T(8,128)S(1)} %convolution_bitcast_fusion), channel_id=1, source_target_pairs={{0,4},{4,8},{8,12},{12,16},{16,20},{20,24},{24,28},{1,5},{5,9},{9,... | collective-permute-start | bytes 12296 | tf_op jit(solution)/shard_map/ppermute | solution.py:10
  21.2 1.3 collective-permute-start.3
  22.5 6.2 %collective-permute-start.4 = (f32[8,128]{1,0:T(8,128)S(1)}, f32[8,128]{1,0:T(8,128)}, u32[]{:S(2)}, u32[]{:S(2)}) collective-permute-start(f32[8,128]{1,0:T(8,128)S(1)} %convolution_bitcast_fusion), channel_id=1, source_target_pairs={{0,8},{4,12},{8,16},{12,20},{16,24},{20,28},{1,9},{5,13},{9,17},{1... | collective-permute-start | bytes 12296 | tf_op jit(solution)/shard_map/ppermute | solution.py:10
  28.7 0.2 convert_element_type.43
  28.9 1.8 %reshape.42 = bf16[8,4608]{1,0:T(8,128)(2,1)} reshape(bf16[8,2,48,48]{3,2,1,0:T(8,128)(2,1)} %param.9) | data formatting | bytes 147456 | tf_op jit(solution)/shard_map/reshape | solution.py:59
  30.7 1.5 %mul.50 = f32[4608]{0:T(1024)} reshape(f32[2,48,48]{2,1,0:T(8,128)} %param.8) | data formatting | bytes 36864 | tf_op jit(solution)/shard_map/mul | solution.py:49
  32.2 7.3 %collective-permute-done = bf16[1,48,48,128]{3,2,1,0:T(8,128)(2,1)} collective-permute-done((bf16[1,48,48,128]{3,2,1,0:T(8,128)(2,1)}, bf16[1,48,48,128]{3,2,1,0:T(8,128)(2,1)}, u32[]{:S(2)}, u32[]{:S(2)}) %collective-permute-start) | collective-permute-done | bytes 589856 | tf_op jit(solution)/shard_map/ppermute | solution.py:18
  39.5 1.3 collective-permute-start.5
  40.8 0.0 collective-permute-done.1
  40.8 1.6 %maximum_convert_fusion = f32[4,48,48,128]{3,2,1,0:T(8,128)S(1)} fusion(bf16[1,48,48,128]{3,2,1,0:T(8,128)(2,1)} %collective-permute-done.1, bf16[2,48,48,128]{3,2,1,0:T(8,128)(2,1)S(1)} %copy-done, bf16[1,48,48,128]{3,2,1,0:T(8,128)(2,1)} %collective-permute-done), kind=kLoop, calls=%fused_computation.34 | loop fusion | flops 3538944 | bytes 7077888 | tf_op jit(solution)/shard_map/convert_element_type | solution.py:37
  42.4 0.0 copy-start.4
  42.4 1.1 fusion.12
  43.5 0.0 copy-done.4
  43.5 0.0 copy-start.1
  43.5 0.0 copy-start.5
  43.5 2.0 %fusion.19 = (f32[4608,128]{1,0:T(8,128)S(1)}, f32[4608,128]{1,0:T(8,128)S(1)}) fusion(f32[2,48,48,128]{3,2,1,0:T(8,128)S(1)} %fusion.12, f32[4608]{0:T(1024)S(1)} %copy-done.4, bf16[2,48,48,128]{3,2,1,0:T(8,128)(2,1)S(1)} %copy-done), kind=kLoop, calls=%fused_computation.38 | loop fusion | flops 2359296 | bytes 8275968 | tf_op jit(solution)/shard_map/add | solution.py:49
  45.6 0.0 collective-permute-done.2
  45.6 0.0 collective-permute-done.3
  45.6 0.0 collective-permute-done.4
  45.6 0.0 collective-permute-done.5
  45.6 0.0 copy-done.1
  45.6 0.0 copy-done.5
  45.6 1.4 %fusion.4 = bf16[4608,128]{1,0:T(8,128)(2,1)S(1)} fusion(f32[4608,128]{1,0:T(8,128)S(1)} %get-tuple-element.8, f32[4608,128]{1,0:T(8,128)S(1)} %get-tuple-element.7, f32[8,128]{1,0:T(8,128)S(1)} %collective-permute-done.5, f32[8,128]{1,0:T(8,128)} %collective-permute-done.4, f32[8,128]{1,0:T(8,128)S(1)} %collective-permute-done.3, ...), kind=kOutput, calls=%fused_computation.6 | convolution fusion | flops 11839488 | bytes 5992488 | tf_op jit(solution)/shard_map/dot_general | solution.py:45
  47.0 0.1 fusion.29
  47.1 4.4 %collective-permute-start.6 = (bf16[1,48,48,128]{3,2,1,0:T(8,128)(2,1)S(1)}, bf16[1,48,48,128]{3,2,1,0:T(8,128)(2,1)S(1)}, u32[]{:S(2)}, u32[]{:S(2)}) collective-permute-start(bf16[1,48,48,128]{3,2,1,0:T(8,128)(2,1)S(1)} %bitcast.34), channel_id=1, source_target_pairs={{0,4},{4,8},{8,12},{12,16},{16,20},{20,24},{24,28},{1,5},{5,9},{9,... | collective-permute-start | bytes 1769480 | tf_op jit(solution)/shard_map/ppermute | solution.py:18
  51.5 1.3 collective-permute-start.7
  52.8 0.3 fusion.28
  53.2 5.6 %collective-permute-start.10 = (f32[8,128]{1,0:T(8,128)S(1)}, f32[8,128]{1,0:T(8,128)S(1)}, u32[]{:S(2)}, u32[]{:S(2)}) collective-permute-start(f32[8,128]{1,0:T(8,128)S(1)} %fusion.28), channel_id=1, source_target_pairs={{0,8},{4,12},{8,16},{12,20},{16,24},{20,28},{1,9},{5,13},{9,17},{1... | collective-permute-start | bytes 12296 | tf_op jit(solution)/shard_map/ppermute | solution.py:10
  58.7 1.3 collective-permute-start.11
  60.0 3.5 %collective-permute-start.8 = (f32[8,128]{1,0:T(8,128)S(1)}, f32[8,128]{1,0:T(8,128)S(1)}, u32[]{:S(2)}, u32[]{:S(2)}) collective-permute-start(f32[8,128]{1,0:T(8,128)S(1)} %fusion.28), channel_id=1, source_target_pairs={{0,4},{4,8},{8,12},{12,16},{16,20},{20,24},{24,28},{1,5},{5,9},{9,... | collective-permute-start | bytes 12296 | tf_op jit(solution)/shard_map/ppermute | solution.py:10
  63.5 0.2 convert_element_type.47
  63.7 12.1 %collective-permute-done.6 = bf16[1,48,48,128]{3,2,1,0:T(8,128)(2,1)S(1)} collective-permute-done((bf16[1,48,48,128]{3,2,1,0:T(8,128)(2,1)S(1)}, bf16[1,48,48,128]{3,2,1,0:T(8,128)(2,1)S(1)}, u32[]{:S(2)}, u32[]{:S(2)}) %collective-permute-start.6) | collective-permute-done | bytes 589856 | tf_op jit(solution)/shard_map/ppermute | solution.py:18
  75.8 1.3 collective-permute-start.9
  77.1 0.0 collective-permute-done.7
  77.1 0.4 maximum_convert_fusion.1
  77.5 0.9 fusion.18
  78.4 0.0 collective-permute-done.10
  78.4 0.0 collective-permute-done.11
  78.4 0.0 collective-permute-done.8
  78.5 3.3 %collective-permute-done.9 = f32[8,128]{1,0:T(8,128)S(1)} collective-permute-done((f32[8,128]{1,0:T(8,128)S(1)}, f32[8,128]{1,0:T(8,128)S(1)}, u32[]{:S(2)}, u32[]{:S(2)}) %collective-permute-start.9) | collective-permute-done | bytes 4128 | tf_op jit(solution)/shard_map/ppermute | solution.py:10
  81.8 0.0 copy-start.6
  81.8 0.0 copy-start.3
  81.8 3.2 %fusion.5 = bf16[4608,128]{1,0:T(8,128)(2,1)} fusion(f32[4608,128]{1,0:T(8,128)S(1)} %bitcast.32, bf16[4608,128]{1,0:T(8,128)(2,1)S(1)} %fusion.4, f32[4608]{0:T(1024)S(1)} %copy-done.4, f32[8,128]{1,0:T(8,128)S(1)} %collective-permute-done.11, f32[8,128]{1,0:T(8,128)S(1)} %collective-permute-done.10, f32[8,128]{1,0:T(8,128)S(1)} %collective-permute-done.9, ...), kind=kOutput, calls=%fused_computation.7 | convolution fusion | flops 14198784 | bytes 4831272 | tf_op jit(solution)/shard_map/dot_general | solution.py:45
  85.0 0.0 all-gather.2.cloned.1.call-update
  85.1 0.0 copy-done.6
  85.1 0.0 copy-done.3
  85.1 0.1 convert_multiply_fusion.2
  85.3 0.3 convolution_convert_fusion.1
  85.6 40.1 %all-gather.2.cloned.1.call-done = bf16[4608,512]{1,0:T(8,128)(2,1)} async-done(((bf16[4608,128]{1,0:T(8,128)(2,1)}), bf16[4608,512]{1,0:T(8,128)(2,1)}) %all-gather.2.cloned.1.call-update) | async-done | bytes 4718608 | tf_op jit(solution)/shard_map/all_gather | solution.py:75
  125.7 4.7 %convolution_convert_fusion = bf16[4608,128]{1,0:T(8,128)(2,1)} fusion(bf16[4608,512]{1,0:T(8,128)(2,1)} %all-gather.2.cloned.1.call-done, bf16[512,128]{1,0:T(8,128)(2,1)S(1)} %bitcast.35), kind=kOutput, calls=%fused_computation.8 | convolution fusion | flops 604569600 | bytes 6029312 | tf_op jit(solution)/shard_map/dot_general | solution.py:74
  (4 shorter events, 0.0 us)
Async XLA Ops:
  6.5 9.5 %copy-start = (bf16[2,48,48,128]{3,2,1,0:T(8,128)(2,1)S(1)}, bf16[2,48,48,128]{3,2,1,0:T(8,128)(2,1)}, u32[]{:S(2)}) copy-start(bf16[2,48,48,128]{3,2,1,0:T(8,128)(2,1)} %param.7) | copy-start | bytes 3538948
  6.5 9.4 %copy-start.7 = (s32[8]{0:T(128)S(1)}, s32[8]{0:T(128)}, u32[]{:S(2)}) copy-start(s32[8]{0:T(128)} %param.11) | copy-start | bytes 100
  6.5 9.4 %copy-start.2 = (bf16[8,2,48,48]{3,2,1,0:T(8,128)(2,1)S(1)}, bf16[8,2,48,48]{3,2,1,0:T(8,128)(2,1)}, u32[]{:S(2)}) copy-start(bf16[8,2,48,48]{3,2,1,0:T(8,128)(2,1)} %param.9) | copy-start | bytes 221188
  6.5 119.2 %all-gather.2.cloned.1.call-start = ((), (), s32[]{:S(2)}) async-start(), calls=%async_computation | async-start | bytes 5898240 | tf_op jit(solution)/shard_map/all_gather | solution.py:75
  9.0 30.5 %collective-permute-start = (bf16[1,48,48,128]{3,2,1,0:T(8,128)(2,1)}, bf16[1,48,48,128]{3,2,1,0:T(8,128)(2,1)}, u32[]{:S(2)}, u32[]{:S(2)}) collective-permute-start(bf16[1,48,48,128]{3,2,1,0:T(8,128)(2,1)} %get-tuple-element.9), channel_id=1, source_target_pairs={{0,4},{4,8},{8,12},{12,16},{16,20},{20,24},{24,28},{1,5},{5,9},{9,... | collective-permute-start | bytes 1769480 | tf_op jit(solution)/shard_map/ppermute | solution.py:18
  14.7 26.1 %collective-permute-start.1 = (bf16[1,48,48,128]{3,2,1,0:T(8,128)(2,1)}, bf16[1,48,48,128]{3,2,1,0:T(8,128)(2,1)}, u32[]{:S(2)}, u32[]{:S(2)}) collective-permute-start(bf16[1,48,48,128]{3,2,1,0:T(8,128)(2,1)} %get-tuple-element.10), channel_id=1, source_target_pairs={{4,0},{8,4},{12,8},{16,12},{20,16},{24,20},{28,24},{5,1},{9,5},{13... | collective-permute-start | bytes 1769480 | tf_op jit(solution)/shard_map/ppermute | solution.py:21
  16.7 28.9 %collective-permute-start.2 = (f32[8,128]{1,0:T(8,128)S(1)}, f32[8,128]{1,0:T(8,128)S(1)}, u32[]{:S(2)}, u32[]{:S(2)}) collective-permute-start(f32[8,128]{1,0:T(8,128)S(1)} %convolution_bitcast_fusion), channel_id=1, source_target_pairs={{0,4},{4,8},{8,12},{12,16},{16,20},{20,24},{24,28},{1,5},{5,9},{9,... | collective-permute-start | bytes 12296 | tf_op jit(solution)/shard_map/ppermute | solution.py:10
  21.2 24.3 %collective-permute-start.3 = (f32[8,128]{1,0:T(8,128)S(1)}, f32[8,128]{1,0:T(8,128)S(1)}, u32[]{:S(2)}, u32[]{:S(2)}) collective-permute-start(f32[8,128]{1,0:T(8,128)S(1)} %convolution_bitcast_fusion), channel_id=1, source_target_pairs={{4,0},{8,4},{12,8},{16,12},{20,16},{24,20},{28,24},{5,1},{9,5},{13... | collective-permute-start | bytes 12296 | tf_op jit(solution)/shard_map/ppermute | solution.py:10
  22.5 23.1 %collective-permute-start.4 = (f32[8,128]{1,0:T(8,128)S(1)}, f32[8,128]{1,0:T(8,128)}, u32[]{:S(2)}, u32[]{:S(2)}) collective-permute-start(f32[8,128]{1,0:T(8,128)S(1)} %convolution_bitcast_fusion), channel_id=1, source_target_pairs={{0,8},{4,12},{8,16},{12,20},{16,24},{20,28},{1,9},{5,13},{9,17},{1... | collective-permute-start | bytes 12296 | tf_op jit(solution)/shard_map/ppermute | solution.py:10
  39.5 6.1 %collective-permute-start.5 = (f32[8,128]{1,0:T(8,128)S(1)}, f32[8,128]{1,0:T(8,128)S(1)}, u32[]{:S(2)}, u32[]{:S(2)}) collective-permute-start(f32[8,128]{1,0:T(8,128)S(1)} %convolution_bitcast_fusion), channel_id=1, source_target_pairs={{8,0},{12,4},{16,8},{20,12},{24,16},{28,20},{9,1},{13,5},{17,9},{2... | collective-permute-start | bytes 12296 | tf_op jit(solution)/shard_map/ppermute | solution.py:10
  42.4 1.1 copy-start.4
  43.5 2.1 %copy-start.1 = (bf16[8,4608]{1,0:T(8,128)(2,1)S(1)}, bf16[8,4608]{1,0:T(8,128)(2,1)}, u32[]{:S(2)}) copy-start(bf16[8,4608]{1,0:T(8,128)(2,1)} %reshape.42) | copy-start | bytes 221188
  43.5 2.1 %copy-start.5 = (f32[8]{0:T(128)S(1)}, f32[8]{0:T(128)}, u32[]{:S(2)}) copy-start(f32[8]{0:T(128)} %param.10) | copy-start | bytes 100
  47.1 28.7 %collective-permute-start.6 = (bf16[1,48,48,128]{3,2,1,0:T(8,128)(2,1)S(1)}, bf16[1,48,48,128]{3,2,1,0:T(8,128)(2,1)S(1)}, u32[]{:S(2)}, u32[]{:S(2)}) collective-permute-start(bf16[1,48,48,128]{3,2,1,0:T(8,128)(2,1)S(1)} %bitcast.34), channel_id=1, source_target_pairs={{0,4},{4,8},{8,12},{12,16},{16,20},{20,24},{24,28},{1,5},{5,9},{9,... | collective-permute-start | bytes 1769480 | tf_op jit(solution)/shard_map/ppermute | solution.py:18
  51.5 25.6 %collective-permute-start.7 = (bf16[1,48,48,128]{3,2,1,0:T(8,128)(2,1)S(1)}, bf16[1,48,48,128]{3,2,1,0:T(8,128)(2,1)S(1)}, u32[]{:S(2)}, u32[]{:S(2)}) collective-permute-start(bf16[1,48,48,128]{3,2,1,0:T(8,128)(2,1)S(1)} %bitcast.33), channel_id=1, source_target_pairs={{4,0},{8,4},{12,8},{16,12},{20,16},{24,20},{28,24},{5,1},{9,5},{13... | collective-permute-start | bytes 1769480 | tf_op jit(solution)/shard_map/ppermute | solution.py:21
  53.2 25.3 %collective-permute-start.10 = (f32[8,128]{1,0:T(8,128)S(1)}, f32[8,128]{1,0:T(8,128)S(1)}, u32[]{:S(2)}, u32[]{:S(2)}) collective-permute-start(f32[8,128]{1,0:T(8,128)S(1)} %fusion.28), channel_id=1, source_target_pairs={{0,8},{4,12},{8,16},{12,20},{16,24},{20,28},{1,9},{5,13},{9,17},{1... | collective-permute-start | bytes 12296 | tf_op jit(solution)/shard_map/ppermute | solution.py:10
  58.7 19.7 %collective-permute-start.11 = (f32[8,128]{1,0:T(8,128)S(1)}, f32[8,128]{1,0:T(8,128)S(1)}, u32[]{:S(2)}, u32[]{:S(2)}) collective-permute-start(f32[8,128]{1,0:T(8,128)S(1)} %fusion.28), channel_id=1, source_target_pairs={{8,0},{12,4},{16,8},{20,12},{24,16},{28,20},{9,1},{13,5},{17,9},{2... | collective-permute-start | bytes 12296 | tf_op jit(solution)/shard_map/ppermute | solution.py:10
  60.0 18.4 %collective-permute-start.8 = (f32[8,128]{1,0:T(8,128)S(1)}, f32[8,128]{1,0:T(8,128)S(1)}, u32[]{:S(2)}, u32[]{:S(2)}) collective-permute-start(f32[8,128]{1,0:T(8,128)S(1)} %fusion.28), channel_id=1, source_target_pairs={{0,4},{4,8},{8,12},{12,16},{16,20},{20,24},{24,28},{1,5},{5,9},{9,... | collective-permute-start | bytes 12296 | tf_op jit(solution)/shard_map/ppermute | solution.py:10
  75.8 6.0 %collective-permute-start.9 = (f32[8,128]{1,0:T(8,128)S(1)}, f32[8,128]{1,0:T(8,128)S(1)}, u32[]{:S(2)}, u32[]{:S(2)}) collective-permute-start(f32[8,128]{1,0:T(8,128)S(1)} %fusion.28), channel_id=1, source_target_pairs={{4,0},{8,4},{12,8},{16,12},{20,16},{24,20},{28,24},{5,1},{9,5},{13... | collective-permute-start | bytes 12296 | tf_op jit(solution)/shard_map/ppermute | solution.py:10
  81.8 3.3 %copy-start.6 = (s32[12,2]{0,1:T(2,128)S(1)}, s32[12,2]{0,1:T(2,128)}, u32[]{:S(2)}) copy-start(s32[12,2]{0,1:T(2,128)} %param.12) | copy-start | bytes 292
  81.8 3.3 %copy-start.3 = (bf16[12,128,128]{2,1,0:T(8,128)(2,1)S(1)}, bf16[12,128,128]{2,1,0:T(8,128)(2,1)}, u32[]{:S(2)}) copy-start(bf16[12,128,128]{2,1,0:T(8,128)(2,1)} %param.13) | copy-start | bytes 1179652
Sparse Core Ops, SparseCore 0:
  85.2 40.5 all-gather.1
where the time goes:
time: 138 us; the launch traced here: 137 us
  waiting for transfers between devices  62.9 us (46%)
  starting transfers between devices  37.6 us (27%)
  between operations  13.7 us (10%)
  matrix products  10.6 us (8%)
  other arithmetic  6.56 us (5%)
  local copies, waits for them, and re-layouts  5.88 us (4%)
    all_gather x1, waiting for transfers between devices, shards(): lax.all_gather(second, 'orb', axis=1, tiled=True)  40.1 us
    ppermute x8, starting transfers between devices, passed_along(): return lax.ppermute(array, axis, pairs)  25 us
    ppermute x2, waiting for transfers between devices, with_halo(): lax.ppermute(lax.slice_in_dim(block, block.shape[dim] - width, None, axis...  19.4 us
    ppermute x2, starting transfers between devices, with_halo(): lax.ppermute(lax.slice_in_dim(block, block.shape[dim] - width, None, axis...  10.1 us
    dot_general x1, matrix products, shards(): jnp.dot(lax.all_gather(second, 'orb', axis=1, tiled=True), column_q, pref...  4.73 us
    dot_general x2, matrix products, apply_filter(): lax.dot_general(beta_m, coef, (((0,), (0,)), ((), ())), preferred_element...  4.63 us
    ppermute x8, waiting for transfers between devices, passed_along(): return lax.ppermute(array, axis, pairs)  3.36 us
  transfers between devices with their start and end apart: 13, of which 4 were waited for; matrix products, arithmetic and copies ran while one was open for 8% of the time, Pallas kernels for 0%

commit v1 on v0

--- a/solution.py
+++ b/solution.py
@@ -2,6 +2,24 @@
 import jax.numpy as jnp
 from jax import lax
 from jax.sharding import PartitionSpec as P
+
+
+def collect(array, axis, dim):
+    ways, here, step = (lax.axis_size(axis), lax.axis_index(axis), array.shape[dim])
+    shape = [n * ways if d == dim else n for d, n in enumerate(array.shape)]
+    full = lax.dynamic_update_slice_in_dim(
+        jnp.zeros(shape, array.dtype), array, here * step, axis=dim
+    )
+    going_up = going_down = array
+    for far in range(1, ways // 2 + 1):
+        going_up = lax.ppermute(going_up, axis, [(d, (d + 1) % ways) for d in range(ways)])
+        full = lax.dynamic_update_slice_in_dim(full, going_up, (here - far) % ways * step, axis=dim)
+        if 2 * far < ways:
+            going_down = lax.ppermute(going_down, axis, [(d, (d - 1) % ways) for d in range(ways)])
+            full = lax.dynamic_update_slice_in_dim(
+                full, going_down, (here + far) % ways * step, axis=dim
+            )
+    return full
 
 
 def passed_along(array, axis, by):
@@ -71,11 +89,7 @@
     mine = (pattern[:, 1] == my_col).astype(jnp.float32)
     column_q = jnp.einsum("ki,k,kab->iab", rows_hot, mine, q_tiles.astype(jnp.float32))
     column_q = column_q.reshape(blocks * tile, tile).astype(jnp.bfloat16)
-    result = jnp.dot(
-        lax.all_gather(second, "orb", axis=1, tiled=True),
-        column_q,
-        preferred_element_type=jnp.float32,
-    )
+    result = jnp.dot(collect(second, "orb", 1), column_q, preferred_element_type=jnp.float32)
     return result.astype(jnp.bfloat16).reshape(planes_z, width_x, width_y, orb_cols)
 
 

time: 138 us -> 132 us (0.957)
  between operations: 13.7 us -> 0.34 us
  local copies, waits for them, and re-layouts: 5.88 us -> 13.8 us
  waiting for transfers between devices: 62.9 us -> 58.5 us
  starting transfers between devices: 37.6 us -> 39.6 us
    all_gather x1 -> x0, waiting for transfers between devices: 40.1 us -> none  [shards(): lax.all_gather(second, 'orb', axis=1, tiled=True)]
    ppermute x0 -> x3, waiting for transfers between devices: none -> 35.5 us  [the longest x2 35.5 us: collect(): lax.ppermute(going_up, axis, [(d, (d + 1) % ways) for d in range(ways)])]
    dynamic_update_slice x0 -> x3, local copies, waits for them, and re-layouts: none -> 3.57 us  [the longest x2 2.37 us: collect(): lax.dynamic_update_slice_in_dim(full, going_up, (here - far) % ways * ste...]
    unnamed x16 -> x22, local copies, waits for them, and re-layouts: 0.03 us -> 2.59 us
    ppermute x0 -> x3, starting transfers between devices: none -> 2.01 us  [the longest x1 1.74 us: collect(): lax.ppermute(going_down, axis, [(d, (d - 1) % ways) for d in range(ways)])]
  transfers between devices with their start and end apart: 13 -> 15, of which waited for: 4 -> 5; matrix products, arithmetic and copies ran while one was open for 8% -> 12% of each run, Pallas kernels for 0% -> 0%
where the time goes in v1:
time: 132 us; the launch traced here: 130 us
  waiting for transfers between devices  58.5 us (44%)
  starting transfers between devices  39.6 us (30%)
  local copies, waits for them, and re-layouts  13.8 us (10%)
  matrix products  10.3 us (8%)
  other arithmetic  7.5 us (6%)
    ppermute x2, waiting for transfers between devices, collect(): lax.ppermute(going_up, axis, [(d, (d + 1) % ways) for d in range(ways)])  35.5 us
    ppermute x8, starting transfers between devices, passed_along(): return lax.ppermute(array, axis, pairs)  25 us
    ppermute x2, waiting for transfers between devices, with_halo(): lax.ppermute(lax.slice_in_dim(block, block.shape[dim] - width, None, axis...  19.7 us
    ppermute x2, starting transfers between devices, with_halo(): lax.ppermute(lax.slice_in_dim(block, block.shape[dim] - width, None, axis...  10.1 us
    dot_general x1, matrix products, shards(): jnp.dot(collect(second, 'orb', 1), column_q, preferred_element_type=jnp.f...  4.74 us
    dot_general x2, matrix products, apply_filter(): lax.dot_general(beta_m, coef, (((0,), (0,)), ((), ())), preferred_element...  4.36 us
    slice x2, local copies, waits for them, and re-layouts, with_halo(): lax.slice_in_dim(block, block.shape[dim] - width, None, axis=dim)  3.34 us
    ppermute x8, waiting for transfers between devices, passed_along(): return lax.ppermute(array, axis, pairs)  3.25 us
  transfers between devices with their start and end apart: 15, of which 5 were waited for; matrix products, arithmetic and copies ran while one was open for 12% of the time, Pallas kernels for 0%

profile of v1, /device:TPU:0, one launch (start us, length us, event | category | flops | bytes accessed | tf_op | source)
XLA Modules:
  0.0 130.0 jit_solution(6738194803823368605)
XLA Ops:
  0.0 2.4 %fusion.30 = (bf16[1,48,48,128]{3,2,1,0:T(8,128)(2,1)}, bf16[1,48,48,128]{3,2,1,0:T(8,128)(2,1)}) fusion(bf16[2,48,48,128]{3,2,1,0:T(8,128)(2,1)} %param.7), kind=kLoop, calls=%fused_computation.63 | loop fusion | bytes 2359296 | tf_op jit(solution)/shard_map/slice | solution.py:37
  2.5 5.7 %collective-permute-start = (bf16[1,48,48,128]{3,2,1,0:T(8,128)(2,1)}, bf16[1,48,48,128]{3,2,1,0:T(8,128)(2,1)}, u32[]{:S(2)}, u32[]{:S(2)}) collective-permute-start(bf16[1,48,48,128]{3,2,1,0:T(8,128)(2,1)} %get-tuple-element.9), channel_id=1, source_target_pairs={{0,4},{4,8},{8,12},{12,16},{16,20},{20,24},{24,28},{1,5},{5,9},{9,... | collective-permute-start | bytes 1769480 | tf_op jit(solution)/shard_map/ppermute | solution.py:36
  8.1 1.3 collective-permute-start.1
  9.4 0.0 copy-done.10
  9.4 0.0 copy-done.3
  9.4 0.1 broadcast_select_fusion
  9.5 0.0 copy-done
  9.5 0.6 convolution_bitcast_fusion
  10.1 4.5 %collective-permute-start.2 = (f32[8,128]{1,0:T(8,128)S(1)}, f32[8,128]{1,0:T(8,128)S(1)}, u32[]{:S(2)}, u32[]{:S(2)}) collective-permute-start(f32[8,128]{1,0:T(8,128)S(1)} %convolution_bitcast_fusion), channel_id=1, source_target_pairs={{0,4},{4,8},{8,12},{12,16},{16,20},{20,24},{24,28},{1,5},{5,9},{9,... | collective-permute-start | bytes 12296 | tf_op jit(solution)/shard_map/ppermute | solution.py:28
  14.7 1.3 collective-permute-start.3
  16.0 6.2 %collective-permute-start.4 = (f32[8,128]{1,0:T(8,128)S(1)}, f32[8,128]{1,0:T(8,128)}, u32[]{:S(2)}, u32[]{:S(2)}) collective-permute-start(f32[8,128]{1,0:T(8,128)S(1)} %convolution_bitcast_fusion), channel_id=1, source_target_pairs={{0,8},{4,12},{8,16},{12,20},{16,24},{20,28},{1,9},{5,13},{9,17},{1... | collective-permute-start | bytes 12296 | tf_op jit(solution)/shard_map/ppermute | solution.py:28
  22.2 0.2 convert_element_type.43
  22.4 1.8 %reshape.42 = bf16[8,4608]{1,0:T(8,128)(2,1)} reshape(bf16[8,2,48,48]{3,2,1,0:T(8,128)(2,1)} %param.9) | data formatting | bytes 147456 | tf_op jit(solution)/shard_map/reshape | solution.py:77
  24.2 1.5 %mul.62 = f32[4608]{0:T(1024)} reshape(f32[2,48,48]{2,1,0:T(8,128)} %param.8) | data formatting | bytes 36864 | tf_op jit(solution)/shard_map/mul | solution.py:67
  25.7 7.3 %collective-permute-done = bf16[1,48,48,128]{3,2,1,0:T(8,128)(2,1)} collective-permute-done((bf16[1,48,48,128]{3,2,1,0:T(8,128)(2,1)}, bf16[1,48,48,128]{3,2,1,0:T(8,128)(2,1)}, u32[]{:S(2)}, u32[]{:S(2)}) %collective-permute-start) | collective-permute-done | bytes 589856 | tf_op jit(solution)/shard_map/ppermute | solution.py:36
  33.0 1.3 collective-permute-start.5
  34.2 0.0 collective-permute-done.1
  34.3 1.6 %maximum_convert_fusion = f32[4,48,48,128]{3,2,1,0:T(8,128)S(1)} fusion(bf16[1,48,48,128]{3,2,1,0:T(8,128)(2,1)} %collective-permute-done.1, bf16[2,48,48,128]{3,2,1,0:T(8,128)(2,1)S(1)} %copy-done, bf16[1,48,48,128]{3,2,1,0:T(8,128)(2,1)} %collective-permute-done), kind=kLoop, calls=%fused_computation.34 | loop fusion | flops 3538944 | bytes 7077888 | tf_op jit(solution)/shard_map/convert_element_type | solution.py:55
  35.9 0.0 copy-start.5
  35.9 1.0 fusion.12
  36.9 0.0 copy-done.5
  36.9 0.0 copy-start.2
  36.9 0.0 copy-start.7
  37.0 2.0 %fusion.19 = (f32[4608,128]{1,0:T(8,128)S(1)}, f32[4608,128]{1,0:T(8,128)S(1)}) fusion(f32[2,48,48,128]{3,2,1,0:T(8,128)S(1)} %fusion.12, f32[4608]{0:T(1024)S(1)} %copy-done.5, bf16[2,48,48,128]{3,2,1,0:T(8,128)(2,1)S(1)} %copy-done), kind=kLoop, calls=%fused_computation.38 | loop fusion | flops 2359296 | bytes 8275968 | tf_op jit(solution)/shard_map/add | solution.py:67
  39.0 0.0 collective-permute-done.2
  39.0 0.0 collective-permute-done.3
  39.0 0.0 collective-permute-done.4
  39.0 0.0 collective-permute-done.5
  39.0 0.0 copy-done.2
  39.0 1.4 %fusion.4 = bf16[4608,128]{1,0:T(8,128)(2,1)S(1)} fusion(f32[4608,128]{1,0:T(8,128)S(1)} %get-tuple-element.8, f32[4608,128]{1,0:T(8,128)S(1)} %get-tuple-element.7, f32[8,128]{1,0:T(8,128)S(1)} %collective-permute-done.5, f32[8,128]{1,0:T(8,128)} %collective-permute-done.4, f32[8,128]{1,0:T(8,128)S(1)} %collective-permute-done.3, ...), kind=kOutput, calls=%fused_computation.6 | convolution fusion | flops 11839488 | bytes 5992488 | tf_op jit(solution)/shard_map/dot_general | solution.py:63
  40.4 0.9 fusion.29
  41.3 4.4 %collective-permute-start.6 = (bf16[1,48,48,128]{3,2,1,0:T(8,128)(2,1)}, bf16[1,48,48,128]{3,2,1,0:T(8,128)(2,1)S(1)}, u32[]{:S(2)}, u32[]{:S(2)}) collective-permute-start(bf16[1,48,48,128]{3,2,1,0:T(8,128)(2,1)} %bitcast.5), channel_id=1, source_target_pairs={{0,4},{4,8},{8,12},{12,16},{16,20},{20,24},{24,28},{1,5},{5,9},{9,... | collective-permute-start | bytes 1769480 | tf_op jit(solution)/shard_map/ppermute | solution.py:36
  45.8 1.3 collective-permute-start.7
  47.1 0.3 fusion.28
  47.4 5.6 %collective-permute-start.10 = (f32[8,128]{1,0:T(8,128)S(1)}, f32[8,128]{1,0:T(8,128)S(1)}, u32[]{:S(2)}, u32[]{:S(2)}) collective-permute-start(f32[8,128]{1,0:T(8,128)S(1)} %fusion.28), channel_id=1, source_target_pairs={{0,8},{4,12},{8,16},{12,20},{16,24},{20,28},{1,9},{5,13},{9,17},{1... | collective-permute-start | bytes 12296 | tf_op jit(solution)/shard_map/ppermute | solution.py:28
  53.0 1.3 collective-permute-start.11
  54.3 3.5 %collective-permute-start.8 = (f32[8,128]{1,0:T(8,128)S(1)}, f32[8,128]{1,0:T(8,128)S(1)}, u32[]{:S(2)}, u32[]{:S(2)}) collective-permute-start(f32[8,128]{1,0:T(8,128)S(1)} %fusion.28), channel_id=1, source_target_pairs={{0,4},{4,8},{8,12},{12,16},{16,20},{20,24},{24,28},{1,5},{5,9},{9,... | collective-permute-start | bytes 12296 | tf_op jit(solution)/shard_map/ppermute | solution.py:28
  57.8 0.2 convert_element_type.47
  57.9 12.4 %collective-permute-done.6 = bf16[1,48,48,128]{3,2,1,0:T(8,128)(2,1)S(1)} collective-permute-done((bf16[1,48,48,128]{3,2,1,0:T(8,128)(2,1)}, bf16[1,48,48,128]{3,2,1,0:T(8,128)(2,1)S(1)}, u32[]{:S(2)}, u32[]{:S(2)}) %collective-permute-start.6) | collective-permute-done | bytes 589856 | tf_op jit(solution)/shard_map/ppermute | solution.py:36
  70.4 1.3 collective-permute-start.9
  71.7 0.0 collective-permute-done.7
  71.7 0.4 maximum_convert_fusion.1
  72.0 0.9 fusion.18
  73.0 0.0 collective-permute-done.10
  73.0 0.0 collective-permute-done.11
  73.0 0.0 collective-permute-done.8
  73.0 3.2 %collective-permute-done.9 = f32[8,128]{1,0:T(8,128)S(1)} collective-permute-done((f32[8,128]{1,0:T(8,128)S(1)}, f32[8,128]{1,0:T(8,128)S(1)}, u32[]{:S(2)}, u32[]{:S(2)}) %collective-permute-start.9) | collective-permute-done | bytes 4128 | tf_op jit(solution)/shard_map/ppermute | solution.py:28
  76.2 0.3 broadcast_in_dim.22
  76.5 0.4 copy-done.6
  77.0 2.9 %constant_dynamic-update-slice_fusion.3 = (bf16[4608,512]{1,0:T(8,128)(2,1)S(1)}, bf16[4608,128]{1,0:T(8,128)(2,1)S(1)}) fusion(bf16[4608,512]{1,0:T(8,128)(2,1)S(1)} %broadcast_in_dim.22, s32[]{:T(128)S(6)} %select_n.36, f32[8,128]{1,0:T(8,128)S(1)} %collective-permute-done.11, f32[8,128]{1,0:T(8,128)S(1)} %collective-permute-done.10, ...), kind=kOutput, calls=%fused_computation.57 | convolution fusion | flops 14198784 | bytes 6013956 | tf_op jit(solution)/shard_map/dot_general | solution.py:63
  79.9 2.1 %copy-done.1 = bf16[4608,512]{1,0:T(8,128)(2,1)} copy-done((bf16[4608,512]{1,0:T(8,128)(2,1)}, bf16[4608,512]{1,0:T(8,128)(2,1)S(1)}, u32[]{:S(2)}) %copy-start.1) | copy-done | bytes 4718616
  82.1 0.0 collective-permute-start.12
  82.1 1.7 %collective-permute-start.13 = (bf16[4608,128]{1,0:T(8,128)(2,1)S(1)}, bf16[4608,128]{1,0:T(8,128)(2,1)S(1)}, u32[]{:S(2)}, u32[]{:S(2)}) collective-permute-start(bf16[4608,128]{1,0:T(8,128)(2,1)S(1)} %get-tuple-element.12), channel_id=1, source_target_pairs={{0,3},{1,0},{2,1},{3,2},{4,7},{5,4},{6,5},{7,6},{8,11},{9,8},{10,9... | collective-permute-start | bytes 3538952 | tf_op jit(solution)/shard_map/ppermute | solution.py:18
  83.8 1.1 convert_multiply_fusion.2
  85.0 0.3 convolution_convert_fusion.1
  85.3 0.7 copy.12
  86.0 22.5 %collective-permute-done.12 = bf16[4608,128]{1,0:T(8,128)(2,1)S(1)} collective-permute-done((bf16[4608,128]{1,0:T(8,128)(2,1)S(1)}, bf16[4608,128]{1,0:T(8,128)(2,1)S(1)}, u32[]{:S(2)}, u32[]{:S(2)}) %collective-permute-start.12) | collective-permute-done | bytes 1179680 | tf_op jit(solution)/shard_map/ppermute | solution.py:15
  108.4 0.3 collective-permute-start.14
  108.7 1.1 constant_dynamic-update-slice_fusion.2
  109.8 0.0 collective-permute-done.13
  109.8 1.2 constant_dynamic-update-slice_fusion.1
  111.1 13.0 %collective-permute-done.14 = bf16[4608,128]{1,0:T(8,128)(2,1)S(1)} collective-permute-done((bf16[4608,128]{1,0:T(8,128)(2,1)S(1)}, bf16[4608,128]{1,0:T(8,128)(2,1)S(1)}, u32[]{:S(2)}, u32[]{:S(2)}) %collective-permute-start.14) | collective-permute-done | bytes 1179680 | tf_op jit(solution)/shard_map/ppermute | solution.py:15
  124.1 1.2 constant_dynamic-update-slice_fusion
  125.3 4.7 %convolution_convert_fusion = bf16[4608,128]{1,0:T(8,128)(2,1)} fusion(bf16[4608,512]{1,0:T(8,128)(2,1)} %constant_dynamic-update-slice_fusion, bf16[512,128]{1,0:T(8,128)(2,1)S(1)} %bitcast.34), kind=kOutput, calls=%fused_computation.8 | convolution fusion | flops 604569600 | bytes 6029312 | tf_op jit(solution)/shard_map/dot_general | solution.py:92
  (15 shorter events, 0.0 us)
Async XLA Ops:
  0.0 9.5 %copy-start = (bf16[2,48,48,128]{3,2,1,0:T(8,128)(2,1)S(1)}, bf16[2,48,48,128]{3,2,1,0:T(8,128)(2,1)}, u32[]{:S(2)}) copy-start(bf16[2,48,48,128]{3,2,1,0:T(8,128)(2,1)} %param.7) | copy-start | bytes 3538948
  0.0 9.4 %copy-start.10 = (s32[8]{0:T(128)S(1)}, s32[8]{0:T(128)}, u32[]{:S(2)}) copy-start(s32[8]{0:T(128)} %param.11) | copy-start | bytes 100
  0.0 9.4 %copy-start.3 = (bf16[8,2,48,48]{3,2,1,0:T(8,128)(2,1)S(1)}, bf16[8,2,48,48]{3,2,1,0:T(8,128)(2,1)}, u32[]{:S(2)}) copy-start(bf16[8,2,48,48]{3,2,1,0:T(8,128)(2,1)} %param.9) | copy-start | bytes 221188
  2.5 30.5 %collective-permute-start = (bf16[1,48,48,128]{3,2,1,0:T(8,128)(2,1)}, bf16[1,48,48,128]{3,2,1,0:T(8,128)(2,1)}, u32[]{:S(2)}, u32[]{:S(2)}) collective-permute-start(bf16[1,48,48,128]{3,2,1,0:T(8,128)(2,1)} %get-tuple-element.9), channel_id=1, source_target_pairs={{0,4},{4,8},{8,12},{12,16},{16,20},{20,24},{24,28},{1,5},{5,9},{9,... | collective-permute-start | bytes 1769480 | tf_op jit(solution)/shard_map/ppermute | solution.py:36
  8.1 26.1 %collective-permute-start.1 = (bf16[1,48,48,128]{3,2,1,0:T(8,128)(2,1)}, bf16[1,48,48,128]{3,2,1,0:T(8,128)(2,1)}, u32[]{:S(2)}, u32[]{:S(2)}) collective-permute-start(bf16[1,48,48,128]{3,2,1,0:T(8,128)(2,1)} %get-tuple-element.10), channel_id=1, source_target_pairs={{4,0},{8,4},{12,8},{16,12},{20,16},{24,20},{28,24},{5,1},{9,5},{13... | collective-permute-start | bytes 1769480 | tf_op jit(solution)/shard_map/ppermute | solution.py:39
  10.1 28.9 %collective-permute-start.2 = (f32[8,128]{1,0:T(8,128)S(1)}, f32[8,128]{1,0:T(8,128)S(1)}, u32[]{:S(2)}, u32[]{:S(2)}) collective-permute-start(f32[8,128]{1,0:T(8,128)S(1)} %convolution_bitcast_fusion), channel_id=1, source_target_pairs={{0,4},{4,8},{8,12},{12,16},{16,20},{20,24},{24,28},{1,5},{5,9},{9,... | collective-permute-start | bytes 12296 | tf_op jit(solution)/shard_map/ppermute | solution.py:28
  14.7 24.3 %collective-permute-start.3 = (f32[8,128]{1,0:T(8,128)S(1)}, f32[8,128]{1,0:T(8,128)S(1)}, u32[]{:S(2)}, u32[]{:S(2)}) collective-permute-start(f32[8,128]{1,0:T(8,128)S(1)} %convolution_bitcast_fusion), channel_id=1, source_target_pairs={{4,0},{8,4},{12,8},{16,12},{20,16},{24,20},{28,24},{5,1},{9,5},{13... | collective-permute-start | bytes 12296 | tf_op jit(solution)/shard_map/ppermute | solution.py:28
  16.0 23.0 %collective-permute-start.4 = (f32[8,128]{1,0:T(8,128)S(1)}, f32[8,128]{1,0:T(8,128)}, u32[]{:S(2)}, u32[]{:S(2)}) collective-permute-start(f32[8,128]{1,0:T(8,128)S(1)} %convolution_bitcast_fusion), channel_id=1, source_target_pairs={{0,8},{4,12},{8,16},{12,20},{16,24},{20,28},{1,9},{5,13},{9,17},{1... | collective-permute-start | bytes 12296 | tf_op jit(solution)/shard_map/ppermute | solution.py:28
  33.0 6.0 %collective-permute-start.5 = (f32[8,128]{1,0:T(8,128)S(1)}, f32[8,128]{1,0:T(8,128)S(1)}, u32[]{:S(2)}, u32[]{:S(2)}) collective-permute-start(f32[8,128]{1,0:T(8,128)S(1)} %convolution_bitcast_fusion), channel_id=1, source_target_pairs={{8,0},{12,4},{16,8},{20,12},{24,16},{28,20},{9,1},{13,5},{17,9},{2... | collective-permute-start | bytes 12296 | tf_op jit(solution)/shard_map/ppermute | solution.py:28
  35.9 1.1 copy-start.5
  36.9 2.1 %copy-start.2 = (bf16[8,4608]{1,0:T(8,128)(2,1)S(1)}, bf16[8,4608]{1,0:T(8,128)(2,1)}, u32[]{:S(2)}) copy-start(bf16[8,4608]{1,0:T(8,128)(2,1)} %reshape.42) | copy-start | bytes 221188
  36.9 2.1 %copy-start.7 = (f32[8]{0:T(128)S(1)}, f32[8]{0:T(128)}, u32[]{:S(2)}) copy-start(f32[8]{0:T(128)} %param.10) | copy-start | bytes 100
  41.3 29.0 %collective-permute-start.6 = (bf16[1,48,48,128]{3,2,1,0:T(8,128)(2,1)}, bf16[1,48,48,128]{3,2,1,0:T(8,128)(2,1)S(1)}, u32[]{:S(2)}, u32[]{:S(2)}) collective-permute-start(bf16[1,48,48,128]{3,2,1,0:T(8,128)(2,1)} %bitcast.5), channel_id=1, source_target_pairs={{0,4},{4,8},{8,12},{12,16},{16,20},{20,24},{24,28},{1,5},{5,9},{9,... | collective-permute-start | bytes 1769480 | tf_op jit(solution)/shard_map/ppermute | solution.py:36
  45.8 25.9 %collective-permute-start.7 = (bf16[1,48,48,128]{3,2,1,0:T(8,128)(2,1)S(1)}, bf16[1,48,48,128]{3,2,1,0:T(8,128)(2,1)S(1)}, u32[]{:S(2)}, u32[]{:S(2)}) collective-permute-start(bf16[1,48,48,128]{3,2,1,0:T(8,128)(2,1)S(1)} %bitcast.33), channel_id=1, source_target_pairs={{4,0},{8,4},{12,8},{16,12},{20,16},{24,20},{28,24},{5,1},{9,5},{13... | collective-permute-start | bytes 1769480 | tf_op jit(solution)/shard_map/ppermute | solution.py:39
  47.4 25.6 %collective-permute-start.10 = (f32[8,128]{1,0:T(8,128)S(1)}, f32[8,128]{1,0:T(8,128)S(1)}, u32[]{:S(2)}, u32[]{:S(2)}) collective-permute-start(f32[8,128]{1,0:T(8,128)S(1)} %fusion.28), channel_id=1, source_target_pairs={{0,8},{4,12},{8,16},{12,20},{16,24},{20,28},{1,9},{5,13},{9,17},{1... | collective-permute-start | bytes 12296 | tf_op jit(solution)/shard_map/ppermute | solution.py:28
  53.0 20.0 %collective-permute-start.11 = (f32[8,128]{1,0:T(8,128)S(1)}, f32[8,128]{1,0:T(8,128)S(1)}, u32[]{:S(2)}, u32[]{:S(2)}) collective-permute-start(f32[8,128]{1,0:T(8,128)S(1)} %fusion.28), channel_id=1, source_target_pairs={{8,0},{12,4},{16,8},{20,12},{24,16},{28,20},{9,1},{13,5},{17,9},{2... | collective-permute-start | bytes 12296 | tf_op jit(solution)/shard_map/ppermute | solution.py:28
  54.3 18.7 %collective-permute-start.8 = (f32[8,128]{1,0:T(8,128)S(1)}, f32[8,128]{1,0:T(8,128)S(1)}, u32[]{:S(2)}, u32[]{:S(2)}) collective-permute-start(f32[8,128]{1,0:T(8,128)S(1)} %fusion.28), channel_id=1, source_target_pairs={{0,4},{4,8},{8,12},{12,16},{16,20},{20,24},{24,28},{1,5},{5,9},{9,... | collective-permute-start | bytes 12296 | tf_op jit(solution)/shard_map/ppermute | solution.py:28
  70.4 5.9 %collective-permute-start.9 = (f32[8,128]{1,0:T(8,128)S(1)}, f32[8,128]{1,0:T(8,128)S(1)}, u32[]{:S(2)}, u32[]{:S(2)}) collective-permute-start(f32[8,128]{1,0:T(8,128)S(1)} %fusion.28), channel_id=1, source_target_pairs={{4,0},{8,4},{12,8},{16,12},{20,16},{24,20},{28,24},{5,1},{9,5},{13... | collective-permute-start | bytes 12296 | tf_op jit(solution)/shard_map/ppermute | solution.py:28
  76.2 0.7 copy-start.6
  76.2 0.7 copy-start.8
  77.0 5.1 %copy-start.9 = (s32[12,2]{0,1:T(2,128)S(1)}, s32[12,2]{0,1:T(2,128)}, u32[]{:S(2)}) copy-start(s32[12,2]{0,1:T(2,128)} %param.12) | copy-start | bytes 292
  79.9 2.1 %copy-start.1 = (bf16[4608,512]{1,0:T(8,128)(2,1)}, bf16[4608,512]{1,0:T(8,128)(2,1)S(1)}, u32[]{:S(2)}) copy-start(bf16[4608,512]{1,0:T(8,128)(2,1)S(1)} %get-tuple-element.11) | copy-start | bytes 14155780
  82.1 26.4 %collective-permute-start.12 = (bf16[4608,128]{1,0:T(8,128)(2,1)S(1)}, bf16[4608,128]{1,0:T(8,128)(2,1)S(1)}, u32[]{:S(2)}, u32[]{:S(2)}) collective-permute-start(bf16[4608,128]{1,0:T(8,128)(2,1)S(1)} %get-tuple-element.12), channel_id=1, source_target_pairs={{0,1},{1,2},{2,3},{3,0},{4,5},{5,6},{6,7},{7,4},{8,9},{9,10},{10,1... | collective-permute-start | bytes 3538952 | tf_op jit(solution)/shard_map/ppermute | solution.py:15
  82.1 27.8 %collective-permute-start.13 = (bf16[4608,128]{1,0:T(8,128)(2,1)S(1)}, bf16[4608,128]{1,0:T(8,128)(2,1)S(1)}, u32[]{:S(2)}, u32[]{:S(2)}) collective-permute-start(bf16[4608,128]{1,0:T(8,128)(2,1)S(1)} %get-tuple-element.12), channel_id=1, source_target_pairs={{0,3},{1,0},{2,1},{3,2},{4,7},{5,4},{6,5},{7,6},{8,11},{9,8},{10,9... | collective-permute-start | bytes 3538952 | tf_op jit(solution)/shard_map/ppermute | solution.py:18
  108.4 15.6 %collective-permute-start.14 = (bf16[4608,128]{1,0:T(8,128)(2,1)S(1)}, bf16[4608,128]{1,0:T(8,128)(2,1)S(1)}, u32[]{:S(2)}, u32[]{:S(2)}) collective-permute-start(bf16[4608,128]{1,0:T(8,128)(2,1)S(1)} %collective-permute-done.12), channel_id=1, source_target_pairs={{0,1},{1,2},{2,3},{3,0},{4,5},{5,6},{6,7},{7,4},{8,9},{9,10},{10,1... | collective-permute-start | bytes 3538952 | tf_op jit(solution)/shard_map/ppermute | solution.py:15
  109.8 15.4 %copy-start.4 = (bf16[4,128,128]{2,1,0:T(8,128)(2,1)S(1)}, bf16[4,128,128]{2,1,0:T(8,128)(2,1)}, u32[]{:S(2)}) copy-start(bf16[4,128,128]{2,1,0:T(8,128)(2,1)} %copy.12) | copy-start | bytes 393220
